TPU v7x, 32 devices: a whole 2x2x4 slice. The times are simulated.
32 devices in a mesh: dp: 16 (over z, y, core), expert: 2 (over x).
Axes of the slice: x: 2, y: 2, z: 4, core: 2. Of those that a mesh axis runs over, the one named last changes fastest.
Arguments:
- tokens: bfloat16 [4096, 2048], P(('dp', 'expert')), may hold values from -6 to 6
- cotangent: bfloat16 [4096, 2048], P(('dp', 'expert')), may hold values from -6 to 6
- expert_ids: int32 [4096, 8], P(('dp', 'expert')), may hold values from 0 to 127, as said below
- route_weights: float32 [4096, 8], P(('dp', 'expert')), may hold values from 0.1 to 1
- join_groups: int32 [16], replicated, may hold values from 0 to 1
- w_gate: bfloat16 [2048, 1024], P('dp', 'expert'), may hold values from -0.125 to 0.125
- w_up: bfloat16 [2048, 1024], P('dp', 'expert'), may hold values from -0.125 to 0.125
- w_down: bfloat16 [2048, 1024], P('dp', 'expert'), may hold values from -0.1875 to 0.1875
Outputs:
- mixed: bfloat16 [4096, 2048], P(('dp', 'expert'))
- grad_gate: bfloat16 [2048, 1024], P('dp', 'expert')
- grad_up: bfloat16 [2048, 1024], P('dp', 'expert')
- grad_down: bfloat16 [2048, 1024], P('dp', 'expert')
Inputs may be any that keep to these rules, and one draw needn't show every extreme that they name: `expert_ids`: each row names 8 different experts; the rows of one device name expert 0 at most 16 times, and the rows of some device exactly 16 times.
All inputs are finite; a program needn't handle non-finite values.
Results may differ from a plain program's by a relative error of at most 0.014.
Values may be sent and summed in bfloat16 or wider, within the bound.
A program may use at most 64 MiB of HBM per device.

v0:
```python
import jax
import jax.numpy as jnp
from jax import lax
from jax.sharding import PartitionSpec as P


def per_device(tokens, cotangent, expert_ids, route_weights, join_groups, w_gate, w_up, w_down):
    highest = lax.Precision.HIGHEST
    tok_count = tokens.shape[0]
    slot_count = tok_count // 8
    slice_width = w_gate.shape[1]
    chosen_mask = expert_ids == 0
    routed = jnp.any(chosen_mask, -1)
    weight = jnp.sum(jnp.where(chosen_mask, route_weights, 0.0), -1)
    places = jnp.cumsum(routed.astype(jnp.int32)) - 1
    slot_ids = jnp.arange(slot_count, dtype=jnp.int32)
    chooser = ((places[None, :] == slot_ids[:, None]) & routed[None, :]).astype(jnp.float32)
    chooser_half = chooser.astype(jnp.bfloat16)
    picked_local = jnp.dot(chooser_half, tokens, preferred_element_type=jnp.float32).astype(
        jnp.bfloat16
    )
    picked = lax.all_gather(picked_local, "expert", axis=0, tiled=True)
    gate_acts = jnp.dot(
        picked, lax.all_gather(w_gate, "dp", axis=0, tiled=True), preferred_element_type=jnp.float32
    )
    up_acts = jnp.dot(
        picked, lax.all_gather(w_up, "dp", axis=0, tiled=True), preferred_element_type=jnp.float32
    )
    hidden = (jax.nn.silu(gate_acts) * up_acts).astype(jnp.bfloat16)
    trans_dims = (((1,), (1,)), ((), ()))
    full_down = lax.all_gather(w_down, "dp", axis=0, tiled=True)
    partial_out = lax.dot_general(hidden, full_down, trans_dims, preferred_element_type=jnp.float32)
    out_rows = lax.psum_scatter(
        partial_out.astype(jnp.bfloat16), "expert", scatter_dimension=0, tiled=True
    ).astype(jnp.float32)
    placed = lax.dot_general(
        chooser,
        out_rows,
        (((0,), (0,)), ((), ())),
        precision=highest,
        preferred_element_type=jnp.float32,
    )
    mixed = (placed * weight[:, None]).astype(jnp.bfloat16)
    scaled = cotangent.astype(jnp.float32) * weight[:, None]
    dpicked_local = jnp.dot(
        chooser, scaled, precision=highest, preferred_element_type=jnp.float32
    ).astype(jnp.bfloat16)
    dpicked = lax.all_gather(dpicked_local, "expert", axis=0, tiled=True)
    hidden_grad = jnp.dot(dpicked, full_down, preferred_element_type=jnp.float32)
    sigma_gate = jax.nn.sigmoid(gate_acts)
    dgate = (hidden_grad * up_acts * sigma_gate * (1.0 + gate_acts * (1.0 - sigma_gate))).astype(
        jnp.bfloat16
    )
    dup = (hidden_grad * gate_acts * sigma_gate).astype(jnp.bfloat16)
    group_total = lax.axis_size("dp")
    mine = jnp.arange(group_total, dtype=jnp.int32) == lax.axis_index("dp")
    active = 1.0 - jnp.sum(jnp.where(mine, join_groups, 0)).astype(jnp.float32)
    col_dims = (((0,), (0,)), ((), ()))

    def term_of(left, right):
        return active * lax.dot_general(left, right, col_dims, preferred_element_type=jnp.float32)

    summed = lax.psum_scatter(
        jnp.concatenate(
            [term_of(picked, dgate), term_of(picked, dup), term_of(dpicked, hidden)], axis=1
        ),
        "dp",
        scatter_dimension=0,
        tiled=True,
    )
    grad_gate = summed[:, :slice_width]
    grad_up = summed[:, slice_width : 2 * slice_width]
    grad_down = summed[:, 2 * slice_width :]
    return (
        mixed,
        grad_gate.astype(jnp.bfloat16),
        grad_up.astype(jnp.bfloat16),
        grad_down.astype(jnp.bfloat16),
    )


def solution(mesh):
    in_specs = (
        P(("dp", "expert"), None),
        P(("dp", "expert"), None),
        P(("dp", "expert"), None),
        P(("dp", "expert"), None),
        P(),
        P("dp", "expert"),
        P("dp", "expert"),
        P("dp", "expert"),
    )
    out_specs = (P(("dp", "expert"), None), P("dp", "expert"), P("dp", "expert"), P("dp", "expert"))
    return jax.shard_map(
        per_device, mesh=mesh, in_specs=in_specs, out_specs=out_specs, check_vma=False
    )
```

profile of v0, /device:TPU:0, one launch (start us, length us, event | category | flops | bytes accessed | tf_op | source)
XLA Modules:
  0.0 300.2 jit_solution(16604740441010829208)
XLA Ops:
  7.2 0.0 copy-start
  7.2 0.0 all-gather.4.cloned.1.call-start
  7.2 0.7 all-gather.4.cloned.1.call-update
  7.9 0.0 all-gather.6.cloned.1.call-start
  8.0 0.7 all-gather.6.cloned.1.call-update
  8.7 0.0 all-gather.8.cloned.1.call-start
  8.7 0.7 all-gather.8.cloned.1.call-update
  9.4 0.0 reduce-scatter.3.cloned.1.call-start
  9.5 1.3 fusion.15
  11.4 0.7 select_reduce_fusion
  12.1 0.1 copy.16
  12.3 0.2 reduce-window.8
  12.4 0.1 add_reduce_fusion
  12.5 1.6 convolution_convert_fusion.1
  14.2 5.9 %all_gather.19 = bf16[32,2048]{1,0:T(8,128)(2,1)S(1)} all-gather(bf16[16,2048]{1,0:T(8,128)(2,1)S(1)} %convolution_convert_fusion.1), channel_id=1, replica_groups=mesh['dp'=16,'expert'=2] {'expert'}, dimensions={0}, use_global_device_ids=true | all-gather | bytes 196608 | tf_op jit(solution)/shard_map/all_gather | solution.py:48
  20.0 0.0 copy-done
  20.0 0.2 convolution_convert_fusion.2
  20.2 4.9 %all_gather.15 = bf16[32,2048]{1,0:T(8,128)(2,1)S(1)} all-gather(bf16[16,2048]{1,0:T(8,128)(2,1)S(1)} %convolution_convert_fusion.2), channel_id=1, replica_groups=mesh['dp'=16,'expert'=2] {'expert'}, dimensions={0}, use_global_device_ids=true | all-gather | bytes 196608 | tf_op jit(solution)/shard_map/all_gather | solution.py:22
  25.1 29.2 %all-gather.4.cloned.1.call-done = bf16[2048,512]{1,0:T(8,128)(2,1)} async-done(((bf16[128,512]{1,0:T(8,128)(2,1)}), bf16[2048,512]{1,0:T(8,128)(2,1)}) %all-gather.4.cloned.1.call-update) | async-done | bytes 2097168 | tf_op jit(solution)/shard_map/all_gather | solution.py:24
  54.4 2.0 fusion.19
  56.4 40.3 %all-gather.6.cloned.1.call-done = bf16[2048,512]{1,0:T(8,128)(2,1)} async-done(((bf16[128,512]{1,0:T(8,128)(2,1)}), bf16[2048,512]{1,0:T(8,128)(2,1)}) %all-gather.6.cloned.1.call-update) | async-done | bytes 2097168 | tf_op jit(solution)/shard_map/all_gather | solution.py:27
  96.7 2.0 multiply_convert_fusion.2
  98.8 40.3 %all-gather.8.cloned.1.call-done = bf16[2048,512]{1,0:T(8,128)(2,1)} async-done(((bf16[128,512]{1,0:T(8,128)(2,1)}), bf16[2048,512]{1,0:T(8,128)(2,1)}) %all-gather.8.cloned.1.call-update) | async-done | bytes 2097168 | tf_op jit(solution)/shard_map/all_gather | solution.py:31
  139.1 0.0 copy-start.1
  139.1 3.1 %convolution_convert_fusion = bf16[32,2048]{1,0:T(8,128)(2,1)} fusion(bf16[32,512]{1,0:T(8,128)(2,1)S(1)} %get-tuple-element.17, bf16[2048,512]{1,0:T(8,128)(2,1)} %all-gather.8.cloned.1.call-done), kind=kOutput, calls=%fused_computation.6 | convolution fusion | flops 67174400 | bytes 2260992 | tf_op jit(solution)/shard_map/dot_general | solution.py:32
  142.2 0.0 reduce-scatter.3.cloned.1.call-update
  142.3 0.0 reduce-scatter.5.cloned.1.call-start
  142.3 0.7 convolution_multiply_fusion
  143.1 0.0 copy-done.1
  143.1 0.5 fusion.20
  143.5 0.8 convolution_multiply_fusion.1
  144.3 0.8 convolution_multiply_fusion.2
  145.1 5.4 %pad_maximum_fusion = f32[2048,1536]{0,1:T(8,128)} fusion(f32[2048,512]{0,1:T(8,128)S(1)} %convolution_multiply_fusion, f32[2048,512]{0,1:T(8,128)S(1)} %convolution_multiply_fusion.1, f32[2048,512]{0,1:T(8,128)S(1)} %convolution_multiply_fusion.2), kind=kLoop, calls=%fused_computation | loop fusion | flops 6291456 | bytes 25165824 | tf_op jit(solution)/shard_map/concatenate | solution.py:64
  150.5 0.0 reduce-scatter.5.cloned.1.call-update
  150.5 1.0 reduce-scatter.3.cloned.1.call-done
  151.5 2.0 fusion
  153.5 136.7 %reduce-scatter.5.cloned.1.call-done = f32[128,1536]{0,1:T(8,128)} async-done(((f32[2048,1536]{0,1:T(8,128)}), f32[128,1536]{0,1:T(8,128)}) %reduce-scatter.5.cloned.1.call-update) | async-done | bytes 786448 | tf_op jit(solution)/shard_map/reduce_scatter | solution.py:63
  290.2 1.2 convert.6
  291.4 0.8 copy.19
  292.2 0.8 copy.18
  292.9 0.8 copy.17
  (3 shorter events, 0.1 us)
Async XLA Ops:
  7.2 12.9 %copy-start = (bf16[128,2048]{1,0:T(8,128)(2,1)S(1)}, bf16[128,2048]{1,0:T(8,128)(2,1)}, u32[]{:S(2)}) copy-start(bf16[128,2048]{1,0:T(8,128)(2,1)} %param.8) | copy-start | bytes 1572868
  7.2 47.2 %all-gather.4.cloned.1.call-start = ((), (), s32[]{:S(2)}) async-start(), calls=%async_computation.2 | async-start | bytes 2228224 | tf_op jit(solution)/shard_map/all_gather | solution.py:24
  7.9 88.8 %all-gather.6.cloned.1.call-start = ((), (), s32[]{:S(2)}) async-start(), calls=%async_computation.3 | async-start | bytes 2228224 | tf_op jit(solution)/shard_map/all_gather | solution.py:27
  8.7 130.4 %all-gather.8.cloned.1.call-start = ((), (), s32[]{:S(2)}) async-start(), calls=%async_computation.4 | async-start | bytes 2228224 | tf_op jit(solution)/shard_map/all_gather | solution.py:31
  9.4 142.1 %reduce-scatter.3.cloned.1.call-start = ((), (), s32[]{:S(2)}) async-start(), calls=%async_computation.5 | async-start | bytes 196608 | tf_op jit(solution)/shard_map/reduce_scatter | solution.py:33
  139.1 4.0 %copy-start.1 = (bf16[2048,512]{1,0:T(8,128)(2,1)S(1)}, bf16[2048,512]{1,0:T(8,128)(2,1)}, u32[]{:S(2)}) copy-start(bf16[2048,512]{1,0:T(8,128)(2,1)} %all-gather.8.cloned.1.call-done) | copy-start | bytes 6291460
  142.3 147.9 %reduce-scatter.5.cloned.1.call-start = ((), (), s32[]{:S(2)}) async-start(), calls=%async_computation.6 | async-start | bytes 13369344 | tf_op jit(solution)/shard_map/reduce_scatter | solution.py:63
Sparse Core Ops, SparseCore 0:
  10.2 44.1 all-gather.3
  56.5 40.1 all-gather.5
  98.9 40.1 all-gather.7
  142.4 9.0 reduce-scatter.2
  155.4 134.7 reduce-scatter.4
where the time goes:
time: 301 us; the launch traced here: 300 us
  waiting for transfers between devices  250 us (83%)
  between operations  14.5 us (5%)
  matrix products  13.7 us (5%)
  blocking collectives  10.8 us (4%)
  other arithmetic  8.91 us (3%)
    reduce_scatter x1, waiting for transfers between devices, per_device(): lax.psum_scatter(jnp.concatenate([term_of(picked, dgate), term_of(picked,...  137 us
    all_gather x1, waiting for transfers between devices, per_device(): full_down = lax.all_gather(w_down, 'dp', axis=0, tiled=True)  40.3 us
    all_gather x1, waiting for transfers between devices, per_device(): lax.all_gather(w_up, 'dp', axis=0, tiled=True)  40.3 us
    all_gather x1, waiting for transfers between devices, per_device(): lax.all_gather(w_gate, 'dp', axis=0, tiled=True)  29.2 us
  transfers between devices with their start and end apart: 5, of which 5 were waited for; matrix products, arithmetic and copies ran while one was open for 6% of the time, Pallas kernels for 0%

commit v1 on v0

--- a/solution.py
+++ b/solution.py
@@ -2,6 +2,18 @@
 import jax.numpy as jnp
 from jax import lax
 from jax.sharding import PartitionSpec as P
+
+
+def collect(x, axis, dim):
+    ways, here, hop = (lax.axis_size(axis), lax.axis_index(axis), x.shape[dim])
+    line, have = (x, 1)
+    while have < ways:
+        line = jnp.concatenate(
+            [line, lax.ppermute(line, axis, [(d, (d - have) % ways) for d in range(ways)])],
+            axis=dim,
+        )
+        have = 2 * have
+    return jnp.roll(line, here * hop, axis=dim)
 
 
 def per_device(tokens, cotangent, expert_ids, route_weights, join_groups, w_gate, w_up, w_down):
@@ -23,9 +35,7 @@
     gate_acts = jnp.dot(
         picked, lax.all_gather(w_gate, "dp", axis=0, tiled=True), preferred_element_type=jnp.float32
     )
-    up_acts = jnp.dot(
-        picked, lax.all_gather(w_up, "dp", axis=0, tiled=True), preferred_element_type=jnp.float32
-    )
+    up_acts = jnp.dot(picked, collect(w_up, "dp", 0), preferred_element_type=jnp.float32)
     hidden = (jax.nn.silu(gate_acts) * up_acts).astype(jnp.bfloat16)
     trans_dims = (((1,), (1,)), ((), ()))
     full_down = lax.all_gather(w_down, "dp", axis=0, tiled=True)

time: 301 us -> 316 us (1.050)
  waiting for transfers between devices: 250 us -> 240 us
  local copies, waits for them, and re-layouts: 2.47 us -> 11.8 us
  starting transfers between devices: 0.19 us -> 8.1 us
  other arithmetic: 8.91 us -> 14.2 us
    ppermute x0 -> x4, waiting for transfers between devices: none -> 65.1 us  [collect(): lax.ppermute(line, axis, [(d, (d - have) % ways) for d in range(ways)])]
    all_gather x1, waiting for transfers between devices: 40.3 us -> 0.01 us  [per_device(): full_down = lax.all_gather(w_down, 'dp', axis=0, tiled=True)]
    all_gather x1 -> x0, waiting for transfers between devices: 40.3 us -> none  [per_device(): lax.all_gather(w_up, 'dp', axis=0, tiled=True)]
    unnamed x7 -> x24, local copies, waits for them, and re-layouts: 2.32 us -> 10.6 us
    all_gather x1, waiting for transfers between devices: 29.2 us -> 37.4 us  [per_device(): lax.all_gather(w_gate, 'dp', axis=0, tiled=True)]
    ppermute x0 -> x4, starting transfers between devices: none -> 7.94 us  [collect(): lax.ppermute(line, axis, [(d, (d - have) % ways) for d in range(ways)])]
    dot_general x3, matrix products: 2.29 us -> 6.18 us  [term_of(): lax.dot_general(left, right, col_dims, preferred_element_type=jnp.float32)]
    concatenate x0 -> x3, other arithmetic: none -> 3.82 us  [collect(): jnp.concatenate([line, lax.ppermute(line, axis, [(d, (d - have) % ways) f...]
  transfers between devices with their start and end apart: 5 -> 8, of which waited for: 5 -> 6; matrix products, arithmetic and copies ran while one was open for 6% -> 8% of each run, Pallas kernels for 0% -> 0%
where the time goes in v1:
time: 316 us; the launch traced here: 315 us
  waiting for transfers between devices  240 us (76%)
  matrix products  16.6 us (5%)
  between operations  14.5 us (5%)
  other arithmetic  14.2 us (4%)
  local copies, waits for them, and re-layouts  11.8 us (4%)
  blocking collectives  9.86 us (3%)
  starting transfers between devices  8.1 us (3%)
    reduce_scatter x1, waiting for transfers between devices, per_device(): lax.psum_scatter(jnp.concatenate([term_of(picked, dgate), term_of(picked,...  136 us
    ppermute x4, waiting for transfers between devices, collect(): lax.ppermute(line, axis, [(d, (d - have) % ways) for d in range(ways)])  65.1 us
    all_gather x1, waiting for transfers between devices, per_device(): lax.all_gather(w_gate, 'dp', axis=0, tiled=True)  37.4 us
    unnamed x24, local copies, waits for them, and re-layouts  10.6 us
    ppermute x4, starting transfers between devices, collect(): lax.ppermute(line, axis, [(d, (d - have) % ways) for d in range(ways)])  7.94 us
    concatenate x1, other arithmetic, per_device(): jnp.concatenate([term_of(picked, dgate), term_of(picked, dup), term_of(dp...  7.55 us
  transfers between devices with their start and end apart: 8, of which 6 were waited for; matrix products, arithmetic and copies ran while one was open for 8% of the time, Pallas kernels for 0%

profile of v1, /device:TPU:0, one launch (start us, length us, event | category | flops | bytes accessed | tf_op | source)
XLA Modules:
  0.0 315.1 jit_solution(14004520559186750636)
XLA Ops:
  7.3 0.7 all-gather.5.cloned.1.call-update
  8.0 0.7 all-gather.3.cloned.1.call-update
  8.7 5.5 %collective-permute-start = (bf16[128,512]{1,0:T(8,128)(2,1)}, bf16[128,512]{1,0:T(8,128)(2,1)S(1)}, u32[]{:S(2)}, u32[]{:S(2)}) collective-permute-start(bf16[128,512]{1,0:T(8,128)(2,1)} %param.14), channel_id=1, source_target_pairs={{0,30},{2,0},{4,2},{6,4},{8,6},{10,8},{12,10},{14,12},{16,14},{18,... | collective-permute-start | bytes 393224 | tf_op jit(solution)/shard_map/ppermute | solution.py:12
  14.3 2.8 collective-permute-done
  17.1 0.9 pad_maximum_fusion.3
  18.0 0.6 collective-permute-start.1
  18.7 7.3 %collective-permute-done.1 = bf16[256,512]{1,0:T(8,128)(2,1)S(1)} collective-permute-done((bf16[256,512]{1,0:T(8,128)(2,1)S(1)}, bf16[256,512]{1,0:T(8,128)(2,1)S(1)}, u32[]{:S(2)}, u32[]{:S(2)}) %collective-permute-start.1) | collective-permute-done | bytes 262176 | tf_op jit(solution)/shard_map/ppermute | solution.py:12
  26.0 0.9 pad_maximum_fusion.2
  26.9 0.1 collective-permute-start.2
  27.0 0.7 select_reduce_fusion
  27.7 0.1 copy.16
  27.9 0.2 reduce-window.8
  28.0 0.1 add_reduce_fusion
  28.1 13.9 %collective-permute-done.2 = bf16[512,512]{1,0:T(8,128)(2,1)S(1)} collective-permute-done((bf16[512,512]{1,0:T(8,128)(2,1)S(1)}, bf16[512,512]{1,0:T(8,128)(2,1)S(1)}, u32[]{:S(2)}, u32[]{:S(2)}) %collective-permute-start.2) | collective-permute-done | bytes 524320 | tf_op jit(solution)/shard_map/ppermute | solution.py:12
  42.1 2.0 pad_maximum_fusion.1
  44.0 1.7 collective-permute-start.3
  45.8 0.6 fusion.17
  47.1 0.6 convolution_convert_fusion.1
  47.6 4.9 %all_gather.15 = bf16[32,2048]{1,0:T(8,128)(2,1)S(1)} all-gather(bf16[16,2048]{1,0:T(8,128)(2,1)S(1)} %convolution_convert_fusion.1), channel_id=1, replica_groups=mesh['dp'=16,'expert'=2] {'expert'}, dimensions={0}, use_global_device_ids=true | all-gather | bytes 196608 | tf_op jit(solution)/shard_map/all_gather | solution.py:58
  52.6 0.2 convolution_convert_fusion.2
  52.8 4.9 %all_gather.12 = bf16[32,2048]{1,0:T(8,128)(2,1)S(1)} all-gather(bf16[16,2048]{1,0:T(8,128)(2,1)S(1)} %convolution_convert_fusion.2), channel_id=1, replica_groups=mesh['dp'=16,'expert'=2] {'expert'}, dimensions={0}, use_global_device_ids=true | all-gather | bytes 196608 | tf_op jit(solution)/shard_map/all_gather | solution.py:34
  57.7 0.7 constant_dynamic-update-slice_fusion.9
  58.3 0.7 constant_dynamic-update-slice_fusion.8
  59.0 0.7 constant_dynamic-update-slice_fusion.7
  59.8 0.8 constant_dynamic-update-slice_fusion.6
  60.6 41.0 %collective-permute-done.3 = bf16[1024,512]{1,0:T(8,128)(2,1)S(1)} collective-permute-done((bf16[1024,512]{1,0:T(8,128)(2,1)}, bf16[1024,512]{1,0:T(8,128)(2,1)S(1)}, u32[]{:S(2)}, u32[]{:S(2)}) %collective-permute-start.3) | collective-permute-done | bytes 1048608 | tf_op jit(solution)/shard_map/ppermute | solution.py:12
  101.6 1.1 constant_dynamic-update-slice_fusion.5
  102.7 0.7 constant_dynamic-update-slice_fusion.4
  103.4 0.7 constant_dynamic-update-slice_fusion.3
  104.0 0.7 constant_dynamic-update-slice_fusion.2
  104.8 0.8 constant_dynamic-update-slice_fusion.1
  105.6 1.1 constant_dynamic-update-slice_fusion
  106.7 2.1 fusion.23
  108.7 37.4 %all-gather.3.cloned.1.call-done = bf16[2048,512]{1,0:T(8,128)(2,1)} async-done(((bf16[128,512]{1,0:T(8,128)(2,1)}), bf16[2048,512]{1,0:T(8,128)(2,1)}) %all-gather.3.cloned.1.call-update) | async-done | bytes 2097168 | tf_op jit(solution)/shard_map/all_gather | solution.py:36
  146.1 2.0 fusion.22
  148.1 2.7 convolution_multiply_fusion.1
  150.9 2.2 multiply_convert_fusion.2
  153.1 2.7 convolution_multiply_fusion
  155.8 1.4 convolution_convert_fusion
  157.2 0.8 convolution_multiply_fusion.2
  158.0 1.4 copy-done.1
  159.4 7.6 %pad_maximum_fusion = f32[2048,1536]{0,1:T(8,128)} fusion(f32[2048,512]{0,1:T(8,128)} %convolution_multiply_fusion, f32[2048,512]{0,1:T(8,128)S(1)} %copy-done.1, f32[2048,512]{0,1:T(8,128)S(1)} %convolution_multiply_fusion.2), kind=kLoop, calls=%fused_computation | loop fusion | flops 6291456 | bytes 25165824 | tf_op jit(solution)/shard_map/concatenate | solution.py:74
  167.0 2.0 fusion
  169.0 136.1 %reduce-scatter.5.cloned.1.call-done = f32[128,1536]{0,1:T(8,128)} async-done(((f32[2048,1536]{0,1:T(8,128)}), f32[128,1536]{0,1:T(8,128)}) %reduce-scatter.5.cloned.1.call-update) | async-done | bytes 786448 | tf_op jit(solution)/shard_map/reduce_scatter | solution.py:73
  305.1 1.2 convert.6
  306.3 0.8 copy.19
  307.1 0.8 copy.18
  307.8 0.8 copy.17
  (22 shorter events, 0.3 us)
Async XLA Ops:
  7.2 45.4 %copy-start = (bf16[128,2048]{1,0:T(8,128)(2,1)S(1)}, bf16[128,2048]{1,0:T(8,128)(2,1)}, u32[]{:S(2)}) copy-start(bf16[128,2048]{1,0:T(8,128)(2,1)} %param.8) | copy-start | bytes 1572868
  7.2 50.5 %copy-start.3 = (bf16[128,512]{1,0:T(8,128)(2,1)S(1)}, bf16[128,512]{1,0:T(8,128)(2,1)}, u32[]{:S(2)}) copy-start(bf16[128,512]{1,0:T(8,128)(2,1)} %param.14) | copy-start | bytes 393220
  7.2 38.6 %copy-start.5 = (s32[16]{0:T(128)S(1)}, s32[16]{0:T(128)}, u32[]{:S(2)}) copy-start(s32[16]{0:T(128)} %param.12) | copy-start | bytes 196
  7.2 39.8 %copy-start.4 = (bf16[128,2048]{1,0:T(8,128)(2,1)S(1)}, bf16[128,2048]{1,0:T(8,128)(2,1)}, u32[]{:S(2)}) copy-start(bf16[128,2048]{1,0:T(8,128)(2,1)} %param.9) | copy-start | bytes 1572868
  7.2 99.4 %all-gather.5.cloned.1.call-start = ((), (), s32[]{:S(2)}) async-start(), calls=%async_computation.3 | async-start | bytes 2228224 | tf_op jit(solution)/shard_map/all_gather | solution.py:41
  7.9 138.2 %all-gather.3.cloned.1.call-start = ((), (), s32[]{:S(2)}) async-start(), calls=%async_computation.2 | async-start | bytes 2228224 | tf_op jit(solution)/shard_map/all_gather | solution.py:36
  8.7 158.3 %reduce-scatter.3.cloned.1.call-start = ((), (), s32[]{:S(2)}) async-start(), calls=%async_computation.4 | async-start | bytes 196608 | tf_op jit(solution)/shard_map/reduce_scatter | solution.py:43
  8.7 8.4 %collective-permute-start = (bf16[128,512]{1,0:T(8,128)(2,1)}, bf16[128,512]{1,0:T(8,128)(2,1)S(1)}, u32[]{:S(2)}, u32[]{:S(2)}) collective-permute-start(bf16[128,512]{1,0:T(8,128)(2,1)} %param.14), channel_id=1, source_target_pairs={{0,30},{2,0},{4,2},{6,4},{8,6},{10,8},{12,10},{14,12},{16,14},{18,... | collective-permute-start | bytes 393224 | tf_op jit(solution)/shard_map/ppermute | solution.py:12
  18.0 8.0 %collective-permute-start.1 = (bf16[256,512]{1,0:T(8,128)(2,1)S(1)}, bf16[256,512]{1,0:T(8,128)(2,1)S(1)}, u32[]{:S(2)}, u32[]{:S(2)}) collective-permute-start(bf16[256,512]{1,0:T(8,128)(2,1)S(1)} %pad_maximum_fusion.3), channel_id=1, source_target_pairs={{0,28},{2,30},{4,0},{6,2},{8,4},{10,6},{12,8},{14,10},{16,12},{18,... | collective-permute-start | bytes 786440 | tf_op jit(solution)/shard_map/ppermute | solution.py:12
  26.9 15.1 %collective-permute-start.2 = (bf16[512,512]{1,0:T(8,128)(2,1)S(1)}, bf16[512,512]{1,0:T(8,128)(2,1)S(1)}, u32[]{:S(2)}, u32[]{:S(2)}) collective-permute-start(bf16[512,512]{1,0:T(8,128)(2,1)S(1)} %pad_maximum_fusion.2), channel_id=1, source_target_pairs={{0,24},{2,26},{4,28},{6,30},{8,0},{10,2},{12,4},{14,6},{16,8},{18,... | collective-permute-start | bytes 1572872 | tf_op jit(solution)/shard_map/ppermute | solution.py:12
  44.0 57.6 %collective-permute-start.3 = (bf16[1024,512]{1,0:T(8,128)(2,1)}, bf16[1024,512]{1,0:T(8,128)(2,1)S(1)}, u32[]{:S(2)}, u32[]{:S(2)}) collective-permute-start(bf16[1024,512]{1,0:T(8,128)(2,1)} %pad_maximum_fusion.1), channel_id=1, source_target_pairs={{0,16},{2,18},{4,20},{6,22},{8,24},{10,26},{12,28},{14,30},{16,0},... | collective-permute-start | bytes 3145736 | tf_op jit(solution)/shard_map/ppermute | solution.py:12
  150.9 4.9 %copy-start.2 = (bf16[2048,512]{1,0:T(8,128)(2,1)S(1)}, bf16[2048,512]{1,0:T(8,128)(2,1)}, u32[]{:S(2)}) copy-start(bf16[2048,512]{1,0:T(8,128)(2,1)} %all-gather.5.cloned.1.call-done) | copy-start | bytes 6291460
  157.2 147.9 %reduce-scatter.5.cloned.1.call-start = ((), (), s32[]{:S(2)}) async-start(), calls=%async_computation.5 | async-start | bytes 13369344 | tf_op jit(solution)/shard_map/reduce_scatter | solution.py:73
  157.2 2.2 copy-start.1
Sparse Core Ops, SparseCore 0:
  10.2 93.1 all-gather.4
  105.6 40.4 all-gather.2
  157.3 9.0 reduce-scatter.2
  170.3 134.7 reduce-scatter.4
